TPU v7x, 32 devices: a whole 2x2x4 slice. The times are simulated.
32 devices in a mesh: groups: 2 (over y), slab: 4 (over z), chan: 4 (over x, core).
Axes of the slice: x: 2, y: 2, z: 4, core: 2. Of those that a mesh axis runs over, the one named last changes fastest.
Arguments:
- field: float32 [64, 8, 512], P('chan', ('groups', 'slab')), parts along dimension 1, may hold values from -6 to 6
- order: int32 [2, 64], replicated, may hold values from 0 to 63, each once within a row
- w_first: bfloat16 [2, 512, 864], P(None, 'chan'), may hold values from -0.21875 to 0.21875
- b_first: bfloat16 [2, 512], P(None, 'chan'), may hold values from -3 to 3
- w_middle: bfloat16 [2, 512, 512], P(None, 'chan'), may hold values from -0.375 to 0.375
- b_middle: bfloat16 [2, 512], P(None, 'chan'), may hold values from -3 to 3
- w_last: bfloat16 [2, 1728, 512], P(None, None, 'chan'), may hold values from -0.078125 to 0.078125
- b_last: bfloat16 [2, 64], replicated, may hold values from -3 to 3
Outputs:
- flowed: float32 [64, 8, 512], P('chan', ('groups', 'slab')), parts along dimension 1
- logscale: float32 [2, 32, 8], P(None, 'chan', ('groups', 'slab')), parts along dimension 2
There are 2 independent parts, one for each index of `groups`. A program takes and returns all parts, laid end to end along the dimension named above; an argument that names none is the same for every part. Nothing has to cross between parts.
Inputs may be any that keep to these rules, and one draw needn't show every extreme that they name: Each row of order names every channel once.
All inputs are finite; a program needn't handle non-finite values.
Results may differ from a plain program's by a relative error of at most 0.0095.
Values may be sent and summed in bfloat16 or wider, within the bound.
A program may use at most 64 MiB of HBM per device.

v0:
```python
import jax
import jax.numpy as jnp
from jax import lax
from jax.sharding import PartitionSpec as P

C = 64
STEPS = 2
NX = 8
NY = 64
NXY = 512
HALF = 32


def padded_2(cells, sides, width):
    for axis, dim in sides:
        count = lax.axis_size(axis)
        ends = count - 1
        head = lax.slice_in_dim(cells, 0, width, axis=dim)
        tail = lax.slice_in_dim(cells, cells.shape[dim] - width, cells.shape[dim], axis=dim)
        cells = jnp.concatenate(
            [
                lax.ppermute(tail, axis, [(i, (i + 1) % count) for i in range(ends)]),
                cells,
                lax.ppermute(head, axis, [((i + 1) % count, i) for i in range(ends)]),
            ],
            axis=dim,
        )
    return cells


def passed_along(block, axis, distance):
    devices = range(lax.axis_size(axis))
    route = [(i - distance, i) for i in devices if i - distance in devices]
    return lax.ppermute(block, axis, route)


def row_columns(padded, depth_off, row_off, depth, rows, width):
    pieces = [
        padded[
            :, depth_off : depth_off + depth, row_off : row_off + rows, col_off : col_off + width
        ]
        for col_off in range(3)
    ]
    return jnp.stack(pieces).reshape(3 * padded.shape[0], depth * rows * width)


def pad_plane(values):
    return jnp.pad(values, ((0, 0), (0, 0), (1, 1), (1, 1)))


def local(field, order, w_first, b_first, w_middle, b_middle, w_last, b_last):
    n_chan = lax.axis_size("chan")
    chan_index = lax.axis_index("chan")
    depth = field.shape[1]
    cells = depth * NX * NY
    share = HALF // n_chan
    units = w_first.shape[1]
    whole = lax.all_gather(field.astype(jnp.bfloat16), "chan", axis=0, tiled=True).astype(
        field.dtype
    )
    records = []
    for section in range(STEPS):
        permuted = jnp.take(whole, order[section], axis=0)
        front = permuted[:HALF]
        back_own = lax.dynamic_slice_in_dim(permuted, HALF + chan_index * share, share, 0).reshape(
            share, cells
        )
        front_bf = front.astype(jnp.bfloat16).reshape(HALF, depth, NX, NY)
        extended = pad_plane(padded_2(front_bf, (("slab", 1),), 1))
        kernel_one = w_first[section].reshape(units, 3, 3, 3 * HALF)
        total = jnp.zeros((units, cells), jnp.float32)
        for depth_off in range(3):
            for row_off in range(3):
                total = total + jnp.dot(
                    kernel_one[:, depth_off, row_off],
                    row_columns(extended, depth_off, row_off, depth, NX, NY),
                    preferred_element_type=jnp.float32,
                )
        hidden_one = jax.nn.relu(total + b_first[section].astype(jnp.float32)[:, None]).astype(
            jnp.bfloat16
        )
        w_two = w_middle[section]
        summed = jnp.dot(
            w_two,
            lax.all_gather(hidden_one, "chan", axis=0, tiled=True),
            preferred_element_type=jnp.float32,
        )
        hidden_two = jax.nn.relu(summed + b_middle[section].astype(jnp.float32)[:, None]).astype(
            jnp.bfloat16
        )
        reordered = (
            w_last[section]
            .reshape(27, 2, n_chan, share, units)
            .transpose(0, 2, 1, 3, 4)
            .reshape(27, C, units)
        )
        kernel_three = (
            reordered.reshape(3, 3, 3, C, units)
            .transpose(0, 1, 3, 2, 4)
            .reshape(3, 3, C, 3 * units)
        )
        hidden_grid = hidden_two.reshape(units, depth, NX, NY)
        flat_pad = pad_plane(hidden_grid)
        stacked = jnp.zeros((3 * C, cells), jnp.float32)
        for row_off in range(3):
            stacked = stacked + jnp.dot(
                kernel_three[:, row_off].reshape(3 * C, 3 * units),
                row_columns(flat_pad, 0, row_off, depth, NX, NY),
                preferred_element_type=jnp.float32,
            )
        parts = lax.psum_scatter(
            stacked.reshape(3, C, depth, NXY).astype(jnp.bfloat16),
            "chan",
            scatter_dimension=1,
            tiled=True,
        ).astype(jnp.float32)
        below = passed_along(parts[0].astype(jnp.bfloat16), "slab", 1).astype(jnp.float32)
        above = passed_along(parts[2].astype(jnp.bfloat16), "slab", -1).astype(jnp.float32)
        lower = jnp.concatenate([below, parts[0][:, : depth - 1]], axis=1)
        upper = jnp.concatenate([parts[2][:, 1:], above], axis=1)
        owned = (lower + parts[1] + upper).reshape(2 * share, cells)
        bias_all = b_last[section].astype(jnp.float32)
        bias_scale = lax.dynamic_slice_in_dim(bias_all, chan_index * share, share, 0)
        bias_shift = lax.dynamic_slice_in_dim(bias_all, HALF + chan_index * share, share, 0)
        shifted = owned[:share] + bias_scale[:, None] + 2.0
        scale = jax.nn.sigmoid(shifted)
        coupled_own = (back_own + owned[share:] + bias_shift[:, None]) * scale
        records.append(jnp.mean(jax.nn.log_sigmoid(shifted).reshape(share, depth, NXY), axis=2))
        coupled_all = lax.all_gather(
            coupled_own.reshape(share, depth, NXY), "chan", axis=0, tiled=True
        )
        whole = jnp.concatenate([front, coupled_all], axis=0)
    flowed = lax.dynamic_slice_in_dim(whole, chan_index * (C // n_chan), C // n_chan, 0)
    return (flowed, jnp.stack(records))


def solution(mesh):
    return jax.shard_map(
        local,
        mesh=mesh,
        in_specs=(
            P("chan", ("groups", "slab"), None),
            P(),
            P(None, "chan", None),
            P(None, "chan"),
            P(None, "chan", None),
            P(None, "chan"),
            P(None, None, "chan"),
            P(),
        ),
        out_specs=(P("chan", ("groups", "slab"), None), P(None, "chan", ("groups", "slab"))),
        check_vma=False,
    )
```

profile of v0, /device:TPU:0, one launch (start us, length us, event | category | flops | bytes accessed | tf_op | source)
XLA Modules:
  0.0 148.5 jit_solution(13568225378600929319)
XLA Ops:
  7.2 0.8 compare_and_fusion
  8.0 0.8 copy.77
  8.7 6.1 %all_gather.15 = bf16[64,1,512]{2,0,1:T(8,128)(2,1)S(1)} all-gather(bf16[16,1,512]{2,0,1:T(8,128)(2,1)S(1)} %copy.77), channel_id=1, replica_groups=mesh['groups'=2,'slab'=4,'chan'=4] {'chan'}, dimensions={0}, use_global_device_ids=true | all-gather | bytes 81920 | tf_op jit(solution)/shard_map/all_gather | solution.py:58
  14.9 0.7 gather_fusion
  15.8 4.1 %collective-permute-start = (bf16[32,1,8,64]{3,2,0,1:T(8,128)(2,1)S(1)}, bf16[32,1,8,64]{3,2,0,1:T(8,128)(2,1)S(1)}, u32[]{:S(2)}, u32[]{:S(2)}) collective-permute-start(bf16[32,1,8,64]{3,2,0,1:T(8,128)(2,1)S(1)} %reshape.318), channel_id=1, source_target_pairs={{0,4},{4,8},{8,12},{1,5},{5,9},{9,13},{2,6},{6,10},{10,14},{3,7},{... | collective-permute-start | bytes 98312 | tf_op jit(solution)/shard_map/ppermute | solution.py:22
  20.0 1.3 collective-permute-start.1
  21.7 0.6 copy-done.7
  22.3 0.5 bitcast_convert_fusion.1
  22.9 3.2 %collective-permute-done.1 = bf16[32,1,8,64]{3,2,0,1:T(8,128)(2,1)S(1)} collective-permute-done((bf16[32,1,8,64]{3,2,0,1:T(8,128)(2,1)S(1)}, bf16[32,1,8,64]{3,2,0,1:T(8,128)(2,1)S(1)}, u32[]{:S(2)}, u32[]{:S(2)}) %collective-permute-start.1) | collective-permute-done | bytes 32800 | tf_op jit(solution)/shard_map/ppermute | solution.py:24
  26.1 0.3 select_maximum_fusion.2
  26.4 0.9 slice_bitcast_fusion.26
  27.3 0.7 slice_bitcast_fusion.24
  29.9 0.6 copy-done.4
  31.1 0.2 convolution_add_fusion.21
  31.5 0.2 convolution_add_fusion.19
  31.7 0.2 convolution_add_fusion.18
  31.9 0.2 convolution_add_fusion.17
  32.4 0.2 convolution_add_fusion.15
  32.6 0.2 fusion.13
  32.8 7.3 %all_gather.16 = bf16[512,512]{0,1:T(8,128)(2,1)S(1)} all-gather(bf16[128,512]{0,1:T(8,128)(2,1)S(1)} %fusion.13), channel_id=1, replica_groups=mesh['groups'=2,'slab'=4,'chan'=4] {'chan'}, dimensions={0}, use_global_device_ids=true | all-gather | bytes 655360 | tf_op jit(solution)/shard_map/all_gather | solution.py:85
  40.1 0.7 copy-done.10
  40.8 0.3 fusion.11
  41.3 0.3 copy.33
  41.8 0.3 copy.32
  42.2 0.3 copy.29
  42.5 0.3 fusion.28
  42.8 0.3 convolution_add_fusion.3
  43.1 1.0 fusion
  44.2 0.6 copy-done.8
  44.8 18.8 %reduce-scatter.3.cloned.1.call-done = bf16[3,16,1,512]{3,1,2,0:T(8,128)(2,1)} async-done(((bf16[3,64,1,512]{3,1,2,0:T(8,128)(2,1)}), bf16[3,16,1,512]{3,1,2,0:T(8,128)(2,1)}) %reduce-scatter.3.cloned.1.call-update) | async-done | bytes 49168 | tf_op jit(solution)/shard_map/reduce_scatter | solution.py:111
  63.6 0.7 slice_bitcast_fusion.89
  64.3 3.4 %collective-permute-start.2 = (bf16[16,1,512]{2,0,1:T(8,128)(2,1)S(1)}, bf16[16,1,512]{2,0,1:T(8,128)(2,1)S(1)}, u32[]{:S(2)}, u32[]{:S(2)}) collective-permute-start(bf16[16,1,512]{2,0,1:T(8,128)(2,1)S(1)} %get-tuple-element.89), channel_id=1, source_target_pairs={{0,4},{4,8},{8,12},{1,5},{5,9},{9,13},{2,6},{6,10},{10,14},{3,7},{... | collective-permute-start | bytes 49160 | tf_op jit(solution)/shard_map/ppermute | solution.py:34
  67.7 1.3 collective-permute-start.3
  69.3 4.1 %collective-permute-done.3 = bf16[16,1,512]{2,0,1:T(8,128)(2,1)S(1)} collective-permute-done((bf16[16,1,512]{2,0,1:T(8,128)(2,1)S(1)}, bf16[16,1,512]{2,0,1:T(8,128)(2,1)S(1)}, u32[]{:S(2)}, u32[]{:S(2)}) %collective-permute-start.3) | collective-permute-done | bytes 16416 | tf_op jit(solution)/shard_map/ppermute | solution.py:34
  73.4 0.7 fusion.54
  74.3 5.4 %all_gather.17 = f32[32,1,512]{2,0,1:T(8,128)S(1)} all-gather(f32[8,1,512]{2,0,1:T(8,128)S(1)} %get-tuple-element.92), channel_id=1, replica_groups=mesh['groups'=2,'slab'=4,'chan'=4] {'chan'}, dimensions={0}, use_global_device_ids=true | all-gather | bytes 81920 | tf_op jit(solution)/shard_map/all_gather | solution.py:129
  79.7 0.7 gather_fusion.1
  80.6 3.4 %collective-permute-start.4 = (bf16[32,1,8,64]{3,2,0,1:T(8,128)(2,1)S(1)}, bf16[32,1,8,64]{3,2,0,1:T(8,128)(2,1)S(1)}, u32[]{:S(2)}, u32[]{:S(2)}) collective-permute-start(bf16[32,1,8,64]{3,2,0,1:T(8,128)(2,1)S(1)} %reshape.333), channel_id=1, source_target_pairs={{0,4},{4,8},{8,12},{1,5},{5,9},{9,13},{2,6},{6,10},{10,14},{3,7},{... | collective-permute-start | bytes 98312 | tf_op jit(solution)/shard_map/ppermute | solution.py:22
  84.0 1.3 collective-permute-start.5
  85.4 0.4 collective-permute-done.4
  85.9 4.3 %collective-permute-done.5 = bf16[32,1,8,64]{3,2,0,1:T(8,128)(2,1)S(1)} collective-permute-done((bf16[32,1,8,64]{3,2,0,1:T(8,128)(2,1)S(1)}, bf16[32,1,8,64]{3,2,0,1:T(8,128)(2,1)S(1)}, u32[]{:S(2)}, u32[]{:S(2)}) %collective-permute-start.5) | collective-permute-done | bytes 32800 | tf_op jit(solution)/shard_map/ppermute | solution.py:24
  90.1 0.3 select_maximum_fusion
  90.4 0.3 slice_bitcast_fusion.2
  93.2 0.2 convolution_add_fusion.13
  93.4 0.2 convolution_add_fusion.12
  94.7 0.2 fusion.12
  95.0 6.7 %all_gather.18 = bf16[512,512]{0,1:T(8,128)(2,1)S(1)} all-gather(bf16[128,512]{0,1:T(8,128)(2,1)S(1)} %fusion.12), channel_id=1, replica_groups=mesh['groups'=2,'slab'=4,'chan'=4] {'chan'}, dimensions={0}, use_global_device_ids=true | all-gather | bytes 655360 | tf_op jit(solution)/shard_map/all_gather | solution.py:85
  101.7 0.7 copy-done.9
  102.3 0.3 fusion.10
  102.9 0.3 copy.39
  103.3 0.3 copy.38
  103.7 0.3 copy.35
  104.0 0.3 fusion.21
  104.3 0.3 convolution_add_fusion.1
  104.7 1.0 fusion.1
  105.7 18.6 %reduce-scatter.5.cloned.1.call-done = bf16[3,16,1,512]{3,1,2,0:T(8,128)(2,1)} async-done(((bf16[3,64,1,512]{3,1,2,0:T(8,128)(2,1)}), bf16[3,16,1,512]{3,1,2,0:T(8,128)(2,1)}) %reduce-scatter.5.cloned.1.call-update) | async-done | bytes 49168 | tf_op jit(solution)/shard_map/reduce_scatter | solution.py:111
  124.4 0.7 slice_bitcast_fusion.86
  125.1 3.4 %collective-permute-start.6 = (bf16[16,1,512]{2,0,1:T(8,128)(2,1)S(1)}, bf16[16,1,512]{2,0,1:T(8,128)(2,1)S(1)}, u32[]{:S(2)}, u32[]{:S(2)}) collective-permute-start(bf16[16,1,512]{2,0,1:T(8,128)(2,1)S(1)} %get-tuple-element.87), channel_id=1, source_target_pairs={{0,4},{4,8},{8,12},{1,5},{5,9},{9,13},{2,6},{6,10},{10,14},{3,7},{... | collective-permute-start | bytes 49160 | tf_op jit(solution)/shard_map/ppermute | solution.py:34
  128.5 1.3 collective-permute-start.7
  129.9 4.2 %collective-permute-done.7 = bf16[16,1,512]{2,0,1:T(8,128)(2,1)S(1)} collective-permute-done((bf16[16,1,512]{2,0,1:T(8,128)(2,1)S(1)}, bf16[16,1,512]{2,0,1:T(8,128)(2,1)S(1)}, u32[]{:S(2)}, u32[]{:S(2)}) %collective-permute-start.7) | collective-permute-done | bytes 16416 | tf_op jit(solution)/shard_map/ppermute | solution.py:34
  134.1 0.7 fusion.53
  135.1 5.4 %all_gather.19 = f32[32,1,512]{2,0,1:T(8,128)S(1)} all-gather(f32[8,1,512]{2,0,1:T(8,128)S(1)} %get-tuple-element.94), channel_id=1, replica_groups=mesh['groups'=2,'slab'=4,'chan'=4] {'chan'}, dimensions={0}, use_global_device_ids=true | all-gather | bytes 81920 | tf_op jit(solution)/shard_map/all_gather | solution.py:129
  140.5 0.6 copy.41
  141.1 0.6 pad_maximum_fusion.24
  (109 shorter events, 8.8 us)
Async XLA Ops:
  7.2 56.4 %reduce-scatter.3.cloned.1.call-start = ((), (), s32[]{:S(2)}) async-start(), calls=%async_computation.2 | async-start | bytes 245760 | tf_op jit(solution)/shard_map/reduce_scatter | solution.py:111
  14.9 6.4 %copy-start.3 = (bf16[2,128,864]{1,2,0:T(8,128)(2,1)S(1)}, bf16[2,128,864]{1,2,0:T(8,128)(2,1)}, u32[]{:S(2)}) copy-start(bf16[2,128,864]{1,2,0:T(8,128)(2,1)} %param.12) | copy-start | bytes 1327108
  15.6 5.8 %copy-start = (bf16[2,1728,128]{2,1,0:T(8,128)(2,1)S(1)}, bf16[2,1728,128]{2,1,0:T(8,128)(2,1)}, u32[]{:S(2)}) copy-start(bf16[2,1728,128]{2,1,0:T(8,128)(2,1)} %param.16) | copy-start | bytes 2654212
  15.7 58.4 %copy-start.1 = (f32[64,1,512]{2,0,1:T(8,128)}, f32[64,1,512]{2,0,1:T(8,128)S(1)}, u32[]{:S(2)}) copy-start(f32[64,1,512]{2,0,1:T(8,128)S(1)} %bitcast_select_fusion.1) | copy-start | bytes 393220
  15.8 5.5 %copy-start.6 = (bf16[2,128]{1,0:T(2,128)(2,1)S(1)}, bf16[2,128]{1,0:T(2,128)(2,1)}, u32[]{:S(2)}) copy-start(bf16[2,128]{1,0:T(2,128)(2,1)} %param.13) | copy-start | bytes 1540
  15.8 7.1 %collective-permute-start = (bf16[32,1,8,64]{3,2,0,1:T(8,128)(2,1)S(1)}, bf16[32,1,8,64]{3,2,0,1:T(8,128)(2,1)S(1)}, u32[]{:S(2)}, u32[]{:S(2)}) collective-permute-start(bf16[32,1,8,64]{3,2,0,1:T(8,128)(2,1)S(1)} %reshape.318), channel_id=1, source_target_pairs={{0,4},{4,8},{8,12},{1,5},{5,9},{9,13},{2,6},{6,10},{10,14},{3,7},{... | collective-permute-start | bytes 98312 | tf_op jit(solution)/shard_map/ppermute | solution.py:22
  20.0 6.2 %collective-permute-start.1 = (bf16[32,1,8,64]{3,2,0,1:T(8,128)(2,1)S(1)}, bf16[32,1,8,64]{3,2,0,1:T(8,128)(2,1)S(1)}, u32[]{:S(2)}, u32[]{:S(2)}) collective-permute-start(bf16[32,1,8,64]{3,2,0,1:T(8,128)(2,1)S(1)} %reshape.318), channel_id=1, source_target_pairs={{4,0},{8,4},{12,8},{5,1},{9,5},{13,9},{6,2},{10,6},{14,10},{7,3},{... | collective-permute-start | bytes 98312 | tf_op jit(solution)/shard_map/ppermute | solution.py:24
  21.6 0.7 copy-start.7
  29.7 0.8 copy-start.4
  29.7 0.9 copy-start.5
  32.8 7.4 %copy-start.11 = (bf16[2,128,512]{2,1,0:T(8,128)(2,1)S(1)}, bf16[2,128,512]{2,1,0:T(8,128)(2,1)}, u32[]{:S(2)}) copy-start(bf16[2,128,512]{2,1,0:T(8,128)(2,1)} %param.14) | copy-start | bytes 786436
  40.1 0.7 copy-start.10
  44.1 80.3 %reduce-scatter.5.cloned.1.call-start = ((), (), s32[]{:S(2)}) async-start(), calls=%async_computation.3 | async-start | bytes 245760 | tf_op jit(solution)/shard_map/reduce_scatter | solution.py:111
  44.2 0.7 copy-start.8
  64.3 4.9 %collective-permute-start.2 = (bf16[16,1,512]{2,0,1:T(8,128)(2,1)S(1)}, bf16[16,1,512]{2,0,1:T(8,128)(2,1)S(1)}, u32[]{:S(2)}, u32[]{:S(2)}) collective-permute-start(bf16[16,1,512]{2,0,1:T(8,128)(2,1)S(1)} %get-tuple-element.89), channel_id=1, source_target_pairs={{0,4},{4,8},{8,12},{1,5},{5,9},{9,13},{2,6},{6,10},{10,14},{3,7},{... | collective-permute-start | bytes 49160 | tf_op jit(solution)/shard_map/ppermute | solution.py:34
  67.7 5.6 %collective-permute-start.3 = (bf16[16,1,512]{2,0,1:T(8,128)(2,1)S(1)}, bf16[16,1,512]{2,0,1:T(8,128)(2,1)S(1)}, u32[]{:S(2)}, u32[]{:S(2)}) collective-permute-start(bf16[16,1,512]{2,0,1:T(8,128)(2,1)S(1)} %get-tuple-element.90), channel_id=1, source_target_pairs={{4,0},{8,4},{12,8},{5,1},{9,5},{13,9},{6,2},{10,6},{14,10},{7,3},{... | collective-permute-start | bytes 49160 | tf_op jit(solution)/shard_map/ppermute | solution.py:34
  74.3 5.4 %slice-start = ((f32[64,1,512]{2,0,1:T(8,128)}), f32[32,1,512]{2,0,1:T(8,128)S(1)}, s32[]{:S(2)}) async-start(f32[64,1,512]{2,0,1:T(8,128)} %copy-done.1), calls=%async_computation.4 | async-start | bytes 131072 | tf_op jit(solution)/shard_map/slice | solution.py:64
  80.4 54.4 %copy-start.2 = (f32[64,1,512]{2,0,1:T(8,128)}, f32[64,1,512]{2,0,1:T(8,128)S(1)}, u32[]{:S(2)}) copy-start(f32[64,1,512]{2,0,1:T(8,128)S(1)} %bitcast_select_fusion) | copy-start | bytes 393220
  80.6 5.3 %collective-permute-start.4 = (bf16[32,1,8,64]{3,2,0,1:T(8,128)(2,1)S(1)}, bf16[32,1,8,64]{3,2,0,1:T(8,128)(2,1)S(1)}, u32[]{:S(2)}, u32[]{:S(2)}) collective-permute-start(bf16[32,1,8,64]{3,2,0,1:T(8,128)(2,1)S(1)} %reshape.333), channel_id=1, source_target_pairs={{0,4},{4,8},{8,12},{1,5},{5,9},{9,13},{2,6},{6,10},{10,14},{3,7},{... | collective-permute-start | bytes 98312 | tf_op jit(solution)/shard_map/ppermute | solution.py:22
  84.0 6.2 %collective-permute-start.5 = (bf16[32,1,8,64]{3,2,0,1:T(8,128)(2,1)S(1)}, bf16[32,1,8,64]{3,2,0,1:T(8,128)(2,1)S(1)}, u32[]{:S(2)}, u32[]{:S(2)}) collective-permute-start(bf16[32,1,8,64]{3,2,0,1:T(8,128)(2,1)S(1)} %reshape.333), channel_id=1, source_target_pairs={{4,0},{8,4},{12,8},{5,1},{9,5},{13,9},{6,2},{10,6},{14,10},{7,3},{... | collective-permute-start | bytes 98312 | tf_op jit(solution)/shard_map/ppermute | solution.py:24
  101.7 0.7 copy-start.9
  125.1 4.8 %collective-permute-start.6 = (bf16[16,1,512]{2,0,1:T(8,128)(2,1)S(1)}, bf16[16,1,512]{2,0,1:T(8,128)(2,1)S(1)}, u32[]{:S(2)}, u32[]{:S(2)}) collective-permute-start(bf16[16,1,512]{2,0,1:T(8,128)(2,1)S(1)} %get-tuple-element.87), channel_id=1, source_target_pairs={{0,4},{4,8},{8,12},{1,5},{5,9},{9,13},{2,6},{6,10},{10,14},{3,7},{... | collective-permute-start | bytes 49160 | tf_op jit(solution)/shard_map/ppermute | solution.py:34
  128.5 5.6 %collective-permute-start.7 = (bf16[16,1,512]{2,0,1:T(8,128)(2,1)S(1)}, bf16[16,1,512]{2,0,1:T(8,128)(2,1)S(1)}, u32[]{:S(2)}, u32[]{:S(2)}) collective-permute-start(bf16[16,1,512]{2,0,1:T(8,128)(2,1)S(1)} %get-tuple-element.88), channel_id=1, source_target_pairs={{4,0},{8,4},{12,8},{5,1},{9,5},{13,9},{6,2},{10,6},{14,10},{7,3},{... | collective-permute-start | bytes 49160 | tf_op jit(solution)/shard_map/ppermute | solution.py:34
  135.1 5.4 %slice-start.1 = ((f32[64,1,512]{2,0,1:T(8,128)}), f32[32,1,512]{2,0,1:T(8,128)S(1)}, s32[]{:S(2)}) async-start(f32[64,1,512]{2,0,1:T(8,128)} %copy-done.2), calls=%async_computation.5 | async-start | bytes 131072 | tf_op jit(solution)/shard_map/slice | solution.py:64
Sparse Core Ops, SparseCore 0:
  44.2 19.3 reduce-scatter.2
  105.8 18.5 reduce-scatter.4
where the time goes:
time: 149 us
  waiting for transfers between devices  53.8 us (36%)
  blocking collectives  31 us (21%)
  starting transfers between devices  19.6 us (13%)
  local copies, waits for them, and re-layouts  16.3 us (11%)
  between operations  14.8 us (10%)
  matrix products  7.5 us (5%)
  other arithmetic  5.64 us (4%)
    reduce_scatter x2, waiting for transfers between devices, local(): lax.psum_scatter(stacked.reshape(3, C, depth, NXY).astype(jnp.bfloat16),...  37.4 us
    all_gather x2, blocking collectives, local(): lax.all_gather(hidden_one, 'chan', axis=0, tiled=True)  14 us
    all_gather x2, blocking collectives, local(): lax.all_gather(coupled_own.reshape(share, depth, NXY), 'chan', axis=0, ti...  10.8 us
    ppermute x4, starting transfers between devices, passed_along(): return lax.ppermute(block, axis, route)  9.35 us
    ppermute x4, waiting for transfers between devices, passed_along(): return lax.ppermute(block, axis, route)  8.4 us
    ppermute x2, starting transfers between devices, padded_2(): lax.ppermute(tail, axis, [(i, (i + 1) % count) for i in range(ends)])  7.54 us
    ppermute x2, waiting for transfers between devices, padded_2(): lax.ppermute(head, axis, [((i + 1) % count, i) for i in range(ends)])  7.52 us
    all_gather x1, blocking collectives, local(): lax.all_gather(field.astype(jnp.bfloat16), 'chan', axis=0, tiled=True)  6.15 us
  transfers between devices with their start and end apart: 10, of which 8 were waited for; matrix products, arithmetic and copies ran while one was open for 1% of the time, Pallas kernels for 0%

commit v1 on v0

v1 whole, which is shorter than its diff:
```python
import jax
import jax.numpy as jnp
from jax import lax
from jax.experimental import pallas as pl
from jax.experimental.pallas import tpu as pltpu
from jax.sharding import PartitionSpec as P

C = 64
HALF = 32
STEPS = 2
NY = 64
NXY = 512
PAD = 128
MESH = pl.DeviceIdType.MESH
F32 = jnp.float32
BF16 = jnp.bfloat16


def kernel(
    field, order, w_first, b_first, w_middle, b_middle, w_last, b_last,
    flowed, logscale,
    field_in, wf, wm, wl, bias1, bias2, bias3, perm,
    whole, xpad, patches, hidden, hpad, patches3, psend, precv,
    back, csend, cgot, fronts, final_send, final,
    load_sem, send_sem, recv_sem, out_sem,
):
    n_chan = lax.axis_size("chan")
    n_slab = lax.axis_size("slab")
    c = lax.axis_index("chan")
    z = lax.axis_index("slab")
    share = HALF // n_chan
    own = C // n_chan
    units = wf.shape[2]
    has = {0: z > 0, 1: None, 2: z < n_slab - 1}

    def peer(dz, j):
        return {"slab": z + dz, "chan": lax.rem(c + j, n_chan)}

    def each_peer(fn):
        @pl.when(z > 0)
        def _():
            for j in range(n_chan):
                fn(-1, j)

        @pl.when(z < n_slab - 1)
        def _():
            for j in range(n_chan):
                fn(1, j)

        for j in range(1, n_chan):
            fn(0, j)

    loads = [pltpu.make_async_copy(field.at[:, 0, :], field_in, load_sem.at[0])]
    loads.append(pltpu.make_async_copy(w_first, wf, load_sem.at[1]))
    loads.append(pltpu.make_async_copy(w_middle, wm, load_sem.at[2]))
    n = 3
    for k in range(STEPS):
        for a in range(3):
            loads.append(
                pltpu.make_async_copy(
                    w_last.at[k, a], wl.at[k, :, pl.ds(a * C, C), :], load_sem.at[n]
                )
            )
            n += 1
    for load in loads:
        load.start()

    barrier = pltpu.get_barrier_semaphore()

    def greet(dz, j):
        pl.semaphore_signal(barrier, inc=1, device_id=peer(dz, j), device_id_type=MESH)

    each_peer(greet)

    for k in range(STEPS):
        row = order[k : k + 1, :]
        hit = (lax.broadcasted_iota(jnp.int32, (C, C), 0) == row).astype(F32)
        perm[k] = hit.T.astype(BF16)
        bias1[k] = jnp.broadcast_to(b_first[k : k + 1, :].astype(F32), (128, units)).T
        bias2[k] = jnp.broadcast_to(b_middle[k : k + 1, :].astype(F32), (128, units)).T
        bias3[k] = jnp.broadcast_to(b_last[k : k + 1, :].astype(F32), (128, C)).T
    for e in range(3):
        xpad[e, :, 0:PAD] = jnp.zeros((3 * HALF, PAD), BF16)
        xpad[e, :, PAD + NXY :] = jnp.zeros((3 * HALF, PAD), BF16)
        hpad[e, :, 0:PAD] = jnp.zeros((units, PAD), BF16)
        hpad[e, :, PAD + NXY :] = jnp.zeros((units, PAD), BF16)
    for a in (0, 2):

        @pl.when(jnp.logical_not(has[a]))
        def _():
            whole[a] = jnp.zeros((C, NXY), BF16)
            cgot[a] = jnp.zeros((n_chan, 2 * share, NXY // 2), BF16)
            for k in range(STEPS):
                precv[k, a] = jnp.zeros((n_chan, 2 * share, NXY), BF16)

    mine = pl.ds(pl.multiple_of(c * own, own), own)
    loads[0].wait()
    whole[1, mine, :] = field_in[...].astype(BF16)

    sides = jnp.where(z > 0, 1, 0) + jnp.where(z < n_slab - 1, 1, 0)
    pl.semaphore_wait(barrier, n_chan - 1 + n_chan * sides)

    def copy(phase, dz, j, src, dst):
        return pltpu.make_async_remote_copy(
            src_ref=src,
            dst_ref=dst,
            send_sem=send_sem.at[phase, 1 - dz, j],
            recv_sem=recv_sem.at[phase, 1 - dz, j],
            device_id=peer(dz, j),
            device_id_type=MESH,
        )

    def arrive(phase, a, j, dst):
        pltpu.make_async_remote_copy(
            src_ref=dst,
            dst_ref=dst,
            send_sem=send_sem.at[phase, a, j],
            recv_sem=recv_sem.at[phase, a, j],
            device_id=peer(0, 1),
            device_id_type=MESH,
        ).wait_recv()

    def each_source(fn):
        for j in range(1, n_chan):
            fn(1, j)

        @pl.when(z > 0)
        def _():
            for j in range(n_chan):
                fn(0, j)

        @pl.when(z < n_slab - 1)
        def _():
            for j in range(n_chan):
                fn(2, j)

    def source(j):
        return lax.rem(c + n_chan - j, n_chan)

    def send_field(dz, j):
        copy(0, dz, j, whole.at[1, mine, :], whole.at[1 - dz, mine, :]).start()

    each_peer(send_field)

    def field_arrives(a, j):
        rows = pl.ds(pl.multiple_of(source(j) * own, own), own)
        arrive(0, a, j, whole.at[a, rows, :])

    each_source(field_arrives)

    y = lax.rem(lax.broadcasted_iota(jnp.int32, (1, NXY), 1), NY)

    def keep(values, e):
        if e == 0:
            return jnp.where(y == NY - 1, 0.0, values)
        if e == 2:
            return jnp.where(y == 0, 0.0, values)
        return values

    def shifted(b, e):
        start = PAD + NY * (b - 1) + (e - 1)
        return slice(start, start + NXY)

    def wide(column):
        return jnp.concatenate([column] * (NXY // 128), axis=1)

    for k in range(STEPS):
        for a in range(3):
            if k == 0:
                plane = whole[a]
            else:
                got = [cgot[a, s].astype(F32) for s in range(n_chan)]
                got = [jnp.concatenate([g[:share], g[share:]], axis=1) for g in got]
                plane = jnp.concatenate([fronts[a]] + got, axis=0).astype(BF16)
            if a == 1:
                permuted = jnp.dot(perm[k], plane, preferred_element_type=F32)
                back[...] = permuted
                front = permuted[:HALF]
            else:
                front = jnp.dot(perm[k, 0:HALF, :], plane, preferred_element_type=F32)
            if k == 0:
                fronts[a] = front
            for e in range(3):
                xpad[e, a * HALF : (a + 1) * HALF, PAD : PAD + NXY] = keep(front, e).astype(BF16)
        for a in range(3):
            for b in range(3):
                for e in range(3):
                    at = ((a * 3 + b) * 3 + e) * HALF
                    patches[at : at + HALF, :] = xpad[e, a * HALF : (a + 1) * HALF, shifted(b, e)]
        if k == 0:
            loads[1].wait()
        total = lax.dot_general(
            wf[k], patches[...], (((0,), (0,)), ((), ())), preferred_element_type=F32
        )
        rows = pl.ds(pl.multiple_of(c * units, units), units)
        hidden[k, rows, :] = jnp.maximum(total + wide(bias1[k]), 0.0).astype(BF16)
        for j in range(1, n_chan):
            copy(1 + k, 0, j, hidden.at[k, rows, :], hidden.at[k, rows, :]).start()
        if k == 0:
            for load in loads[2:]:
                load.wait()
        summed = jnp.dot(wm[k, :, rows], hidden[k, rows, :], preferred_element_type=F32)
        for j in range(1, n_chan):
            theirs = pl.ds(pl.multiple_of(source(j) * units, units), units)
            arrive(1 + k, 1, j, hidden.at[k, theirs, :])
            summed += jnp.dot(wm[k, :, theirs], hidden[k, theirs, :], preferred_element_type=F32)
        two = jnp.maximum(summed + wide(bias2[k]), 0.0)
        for e in range(3):
            hpad[e, :, PAD : PAD + NXY] = keep(two, e).astype(BF16)
        for b in range(3):
            for e in range(3):
                at = (b * 3 + e) * units
                patches3[at : at + units, :] = hpad[e, :, shifted(b, e)]
        weights = jnp.concatenate([wl[k, i] for i in range(9)], axis=1)
        parts = jnp.dot(weights, patches3[...], preferred_element_type=F32)
        for s in range(n_chan):
            for a in range(3):
                low = a * C + s * share
                psend[k, s, a] = jnp.concatenate(
                    [parts[low : low + share], parts[low + HALF : low + HALF + share]], axis=0
                ).astype(BF16)

        def send_parts(dz, j):
            to = lax.rem(c + j, n_chan)
            copy(3 + k, dz, j, psend.at[k, to, 1 - dz], precv.at[k, 1 - dz, c]).start()

        each_peer(send_parts)
        precv[k, 1, c] = psend[k, c, 1]

        def parts_arrive(a, j):
            arrive(3 + k, a, j, precv.at[k, a, source(j)])

        each_source(parts_arrive)
        net = precv[k, 1, 0].astype(F32)
        for a in range(3):
            for s in range(n_chan):
                if (a, s) != (1, 0):
                    net = net + precv[k, a, s].astype(F32)
        scales = pl.ds(pl.multiple_of(c * share, share), share)
        shifts = pl.ds(pl.multiple_of(HALF + c * share, share), share)
        arg = net[:share] + wide(bias3[k, scales, :]) + 2.0
        coupled = (back[shifts, :] + net[share:] + wide(bias3[k, shifts, :])) * jax.nn.sigmoid(arg)
        if k == 0:
            packed = jnp.concatenate([coupled[:, : NXY // 2], coupled[:, NXY // 2 :]], axis=0)
            csend[...] = packed.astype(BF16)

            def send_coupled(dz, j):
                copy(5, dz, j, csend, cgot.at[1 - dz, c]).start()

            each_peer(send_coupled)
            cgot[1, c] = packed.astype(BF16)
        else:
            final_send[...] = coupled
            keeper = n_chan // 2 + c // 2
            place = pl.ds(pl.multiple_of(lax.rem(c, 2) * share, share), share)
            last = pltpu.make_async_remote_copy(
                src_ref=final_send,
                dst_ref=final.at[place, :],
                send_sem=send_sem.at[6, 1, 0],
                recv_sem=recv_sem.at[6, 1, lax.rem(c, 2)],
                device_id={"chan": keeper},
                device_id_type=MESH,
            )

            @pl.when(keeper != c)
            def _():
                last.start()

            @pl.when(keeper == c)
            def _():
                final[place, :] = coupled

        soft = jnp.minimum(arg, 0.0) - jnp.log1p(jnp.exp(-jnp.abs(arg)))
        means = jnp.broadcast_to(jnp.sum(soft, axis=1, keepdims=True) * (1.0 / NXY), (share, share))
        diagonal = lax.broadcasted_iota(jnp.int32, (share, share), 0) == lax.broadcasted_iota(
            jnp.int32, (share, share), 1
        )
        logscale[k] = jnp.sum(jnp.where(diagonal, means, 0.0), axis=0, keepdims=True)
        if k == 0:

            def coupled_arrives(a, j):
                arrive(5, a, j, cgot.at[a, source(j)])

            each_source(coupled_arrives)

    for i in range(2):
        sender = 2 * (c - n_chan // 2) + i
        place = slice(i * share, (i + 1) * share)

        @pl.when(jnp.logical_and(c >= n_chan // 2, sender != c))
        def _():
            pltpu.make_async_remote_copy(
                src_ref=final_send,
                dst_ref=final.at[place, :],
                send_sem=send_sem.at[6, 1, 0],
                recv_sem=recv_sem.at[6, 1, i],
                device_id=peer(0, 1),
                device_id_type=MESH,
            ).wait_recv()

    @pl.when(c < n_chan // 2)
    def _():
        at = pl.ds(pl.multiple_of(lax.rem(c, 2) * own, own), own)
        final[...] = back[at, :]

    out = pltpu.make_async_copy(final, flowed.at[:, 0, :], out_sem)
    out.start()

    each_peer(lambda dz, j: copy(0, dz, j, whole.at[1, mine, :], whole.at[1 - dz, mine, :]).wait_send())
    for k in range(STEPS):
        rows = pl.ds(pl.multiple_of(c * units, units), units)
        for j in range(1, n_chan):
            copy(1 + k, 0, j, hidden.at[k, rows, :], hidden.at[k, rows, :]).wait_send()
        each_peer(
            lambda dz, j: copy(
                3 + k, dz, j, psend.at[k, lax.rem(c + j, n_chan), 1 - dz], precv.at[k, 1 - dz, c]
            ).wait_send()
        )
    each_peer(lambda dz, j: copy(5, dz, j, csend, cgot.at[1 - dz, c]).wait_send())

    @pl.when(n_chan // 2 + c // 2 != c)
    def _():
        last.wait_send()

    out.wait()


def local(field, order, w_first, b_first, w_middle, b_middle, w_last, b_last):
    n_chan = lax.axis_size("chan")
    share = HALF // n_chan
    own = C // n_chan
    units = w_first.shape[1]
    vmem = pl.BlockSpec(memory_space=pltpu.VMEM)
    hbm = pl.BlockSpec(memory_space=pl.ANY)
    flowed, logscale = pl.pallas_call(
        kernel,
        out_shape=(
            jax.ShapeDtypeStruct(field.shape, F32),
            jax.ShapeDtypeStruct((STEPS, 1, share), F32),
        ),
        in_specs=[hbm, vmem, hbm, vmem, hbm, vmem, hbm, vmem],
        out_specs=(hbm, vmem),
        scratch_shapes=[
            pltpu.VMEM((own, NXY), F32),
            pltpu.VMEM((STEPS, 27 * HALF, units), BF16),
            pltpu.VMEM(w_middle.shape, BF16),
            pltpu.VMEM((STEPS, 9, 3 * C, units), BF16),
            pltpu.VMEM((STEPS, units, 128), F32),
            pltpu.VMEM((STEPS, units, 128), F32),
            pltpu.VMEM((STEPS, C, 128), F32),
            pltpu.VMEM((STEPS, C, C), BF16),
            pltpu.VMEM((3, C, NXY), BF16),
            pltpu.VMEM((3, 3 * HALF, NXY + 2 * PAD), BF16),
            pltpu.VMEM((27 * HALF, NXY), BF16),
            pltpu.VMEM((STEPS, n_chan * units, NXY), BF16),
            pltpu.VMEM((3, units, NXY + 2 * PAD), BF16),
            pltpu.VMEM((9 * units, NXY), BF16),
            pltpu.VMEM((STEPS, n_chan, 3, 2 * share, NXY), BF16),
            pltpu.VMEM((STEPS, 3, n_chan, 2 * share, NXY), BF16),
            pltpu.VMEM((C, NXY), F32),
            pltpu.VMEM((2 * share, NXY // 2), BF16),
            pltpu.VMEM((3, n_chan, 2 * share, NXY // 2), BF16),
            pltpu.VMEM((3, HALF, NXY), F32),
            pltpu.VMEM((share, NXY), F32),
            pltpu.VMEM((own, NXY), F32),
            pltpu.SemaphoreType.DMA((9,)),
            pltpu.SemaphoreType.DMA((7, 3, n_chan)),
            pltpu.SemaphoreType.DMA((7, 3, n_chan)),
            pltpu.SemaphoreType.DMA,
        ],
        compiler_params=pltpu.CompilerParams(
            collective_id=0, has_side_effects=True, vmem_limit_bytes=48 << 20
        ),
    )(
        field, order, jnp.swapaxes(w_first, 1, 2), b_first, w_middle, b_middle,
        w_last.reshape(STEPS, 3, 9, C, units), b_last,
    )
    return flowed, jnp.swapaxes(logscale, 1, 2)


def solution(mesh):
    return jax.shard_map(
        local,
        mesh=mesh,
        in_specs=(
            P("chan", ("groups", "slab"), None),
            P(),
            P(None, "chan", None),
            P(None, "chan"),
            P(None, "chan", None),
            P(None, "chan"),
            P(None, None, "chan"),
            P(),
        ),
        out_specs=(P("chan", ("groups", "slab"), None), P(None, "chan", ("groups", "slab"))),
        check_vma=False,
    )
```

time: 149 us -> 46 us (0.31)
  waiting for transfers between devices: 53.8 us -> 0 us
  Pallas kernels: 0 us -> 39.2 us
  blocking collectives: 31 us -> 0 us
  starting transfers between devices: 19.6 us -> 0 us
  between operations: 14.8 us -> 0.68 us
  local copies, waits for them, and re-layouts: 16.3 us -> 5.75 us
  matrix products: 7.5 us -> 0 us
  other arithmetic: 5.64 us -> 0 us
    pallas_call x0 -> x1, Pallas kernels: none -> 39.2 us  [local(): pl.pallas_call(kernel, out_shape=(jax.ShapeDtypeStruct(field.shape, F32),...]
    reduce_scatter x2 -> x0, waiting for transfers between devices: 37.4 us -> none  [local(): lax.psum_scatter(stacked.reshape(3, C, depth, NXY).astype(jnp.bfloat16),...]
    all_gather x5 -> x0, blocking collectives: 31 us -> none  [the longest x2 14 us: local(): lax.all_gather(hidden_one, 'chan', axis=0, tiled=True)]
    ppermute x8 -> x0, starting transfers between devices: 19.5 us -> none  [the longest x4 9.35 us: passed_along(): return lax.ppermute(block, axis, route)]
    ppermute x8 -> x0, waiting for transfers between devices: 16.3 us -> none  [the longest x4 8.4 us: passed_along(): return lax.ppermute(block, axis, route)]
    dot_general x26 -> x0, matrix products: 7.5 us -> none  [the longest x18 3.78 us: local(): jnp.dot(kernel_one[:, depth_off, row_off], row_columns(extended, depth_of...]
    another operation x14 -> x0, local copies, waits for them, and re-layouts: 4.75 us -> none  [row_columns(): return jnp.stack(pieces).reshape(3 * padded.shape[0], depth * rows * width)]
    reshape x22 -> x0, local copies, waits for them, and re-layouts: 3.58 us -> none  [the longest x18 3.21 us: row_columns(): return jnp.stack(pieces).reshape(3 * padded.shape[0], depth * rows * width)]
  transfers between devices with their start and end apart: 10 -> 0, of which waited for: 8 -> 0; matrix products, arithmetic and copies ran while one was open for 1% -> 0% of each run, Pallas kernels for 0% -> 0%
where the time goes in v1:
time: 46 us; the launch traced here: 45.7 us
  Pallas kernels  39.2 us (85%)
  local copies, waits for them, and re-layouts  5.75 us (12%)
  between operations  0.68 us (1%)
    pallas_call x1, Pallas kernels, local(): pl.pallas_call(kernel, out_shape=(jax.ShapeDtypeStruct(field.shape, F32),...  39.2 us
    unnamed x18, local copies, waits for them, and re-layouts  5.75 us

profile of v1, /device:TPU:0, one launch (start us, length us, event | category | flops | bytes accessed | tf_op | source)
XLA Modules:
  0.0 45.7 jit_solution(17868316252457680507)
XLA Ops:
  0.6 0.0 copy-start.6
  0.6 0.0 copy-start.7
  0.7 0.0 copy-start.4
  0.7 0.0 copy-start.5
  0.7 0.6 %copy-done.6 = bf16[2,128]{1,0:T(2,128)(2,1)S(1)} copy-done((bf16[2,128]{1,0:T(2,128)(2,1)S(1)}, bf16[2,128]{1,0:T(2,128)(2,1)}, u32[]{:S(2)}) %copy-start.6) | copy-done | bytes 536
  1.3 0.0 copy-done.7
  1.3 0.0 copy-done.4
  1.3 0.0 copy-done.5
  1.3 0.0 copy-start
  1.3 1.2 %copy-done = bf16[2,1728,128]{2,1,0:T(8,128)(2,1)S(1)} copy-done((bf16[2,1728,128]{2,1,0:T(8,128)(2,1)S(1)}, bf16[2,1728,128]{2,1,0:T(8,128)(2,1)}, u32[]{:S(2)}) %copy-start) | copy-done | bytes 884760
  2.5 0.0 copy-start.1
  2.5 1.0 %copy-done.1 = bf16[2,128,864]{1,2,0:T(8,128)(2,1)S(1)} copy-done((bf16[2,128,864]{1,2,0:T(8,128)(2,1)S(1)}, bf16[2,128,864]{1,2,0:T(8,128)(2,1)}, u32[]{:S(2)}) %copy-start.1) | copy-done | bytes 442392
  3.5 0.0 copy-start.2
  3.5 0.9 %copy-done.2 = bf16[2,128,512]{2,1,0:T(8,128)(2,1)S(1)} copy-done((bf16[2,128,512]{2,1,0:T(8,128)(2,1)S(1)}, bf16[2,128,512]{2,1,0:T(8,128)(2,1)}, u32[]{:S(2)}) %copy-start.2) | copy-done | bytes 262168
  4.5 0.0 copy-start.3
  4.5 0.8 %copy-done.3 = f32[16,1,512]{2,1,0:T(1,128)S(1)} copy-done((f32[16,1,512]{2,1,0:T(1,128)S(1)}, f32[16,1,512]{2,1,0:T(1,128)}, u32[]{:S(2)}) %copy-start.3) | copy-done | bytes 32792
  5.2 39.2 %shard_map.95 = (f32[16,1,512]{2,1,0:T(1,128)S(1)}, f32[2,1,8]{2,1,0:T(1,128)S(1)}) custom-call(f32[16,1,512]{2,1,0:T(1,128)S(1)} %copy-done.3, s32[2,64]{1,0:T(2,128)S(1)} %copy-done.4, bf16[2,864,128]{2,1,0:T(8,128)(2,1)S(1)} %bitcast.6, bf16[2,128]{1,0:T(2,128)(2,1)S(1)} %copy-done.5, bf16[2,128,512]{2,1,0:T(8,128)(2,1)S(1)} %copy-done.2, ...), custom_call_target="tpu_custom_call" | custom-call | tf_op jit(solution)/shard_map/pallas_call | solution.py:335
  44.5 0.6 %copy.13 = f32[16,1,512]{2,1,0:T(1,128)} copy(f32[16,1,512]{2,1,0:T(1,128)S(1)} %get-tuple-element.10) | data formatting | bytes 65536
  45.1 0.6 %copy.14 = f32[2,8,1]{1,2,0:T(1,128)} copy(f32[2,8,1]{1,2,0:T(1,128)S(1)} %bitcast.7) | data formatting | bytes 128
Async XLA Ops:
  0.6 0.7 %copy-start.6 = (bf16[2,128]{1,0:T(2,128)(2,1)S(1)}, bf16[2,128]{1,0:T(2,128)(2,1)}, u32[]{:S(2)}) copy-start(bf16[2,128]{1,0:T(2,128)(2,1)} %b_middle.1) | copy-start | bytes 1540
  0.6 0.7 %copy-start.7 = (bf16[2,64]{1,0:T(2,128)(2,1)S(1)}, bf16[2,64]{1,0:T(2,128)(2,1)}, u32[]{:S(2)}) copy-start(bf16[2,64]{1,0:T(2,128)(2,1)} %b_last.1) | copy-start | bytes 772
  0.7 0.7 %copy-start.4 = (s32[2,64]{1,0:T(2,128)S(1)}, s32[2,64]{1,0:T(2,128)}, u32[]{:S(2)}) copy-start(s32[2,64]{1,0:T(2,128)} %order.1) | copy-start | bytes 1540
  0.7 0.7 %copy-start.5 = (bf16[2,128]{1,0:T(2,128)(2,1)S(1)}, bf16[2,128]{1,0:T(2,128)(2,1)}, u32[]{:S(2)}) copy-start(bf16[2,128]{1,0:T(2,128)(2,1)} %b_first.1) | copy-start | bytes 1540
  1.3 1.2 %copy-start = (bf16[2,1728,128]{2,1,0:T(8,128)(2,1)S(1)}, bf16[2,1728,128]{2,1,0:T(8,128)(2,1)}, u32[]{:S(2)}) copy-start(bf16[2,1728,128]{2,1,0:T(8,128)(2,1)} %param.14) | copy-start | bytes 2654212
  2.5 1.0 %copy-start.1 = (bf16[2,128,864]{1,2,0:T(8,128)(2,1)S(1)}, bf16[2,128,864]{1,2,0:T(8,128)(2,1)}, u32[]{:S(2)}) copy-start(bf16[2,128,864]{1,2,0:T(8,128)(2,1)} %param.10) | copy-start | bytes 1327108
  3.5 0.9 %copy-start.2 = (bf16[2,128,512]{2,1,0:T(8,128)(2,1)S(1)}, bf16[2,128,512]{2,1,0:T(8,128)(2,1)}, u32[]{:S(2)}) copy-start(bf16[2,128,512]{2,1,0:T(8,128)(2,1)} %w_middle.1) | copy-start | bytes 786436
  4.5 0.8 %copy-start.3 = (f32[16,1,512]{2,1,0:T(1,128)S(1)}, f32[16,1,512]{2,1,0:T(1,128)}, u32[]{:S(2)}) copy-start(f32[16,1,512]{2,1,0:T(1,128)} %field.1) | copy-start | bytes 98308

commit v2 on v1

--- a/solution.py
+++ b/solution.py
@@ -25,6 +25,7 @@
     load_sem, send_sem, recv_sem, out_sem,
 ):
     n_chan = lax.axis_size("chan")
+    assert n_chan == 4
     n_slab = lax.axis_size("slab")
     c = lax.axis_index("chan")
     z = lax.axis_index("slab")
@@ -33,10 +34,15 @@
     units = wf.shape[2]
     has = {0: z > 0, 1: None, 2: z < n_slab - 1}
 
+    place_of = (c, c + 1 - 2 * lax.rem(c, 2), lax.rem(c + 2, 4), 3 - c)
+
     def peer(dz, j):
-        return {"slab": z + dz, "chan": lax.rem(c + j, n_chan)}
+        return {"slab": z + dz, "chan": place_of[j]}
 
     def each_peer(fn):
+        for j in (2, 3, 1):
+            fn(0, j)
+
         @pl.when(z > 0)
         def _():
             for j in range(n_chan):
@@ -46,9 +52,6 @@
         def _():
             for j in range(n_chan):
                 fn(1, j)
-
-        for j in range(1, n_chan):
-            fn(0, j)
 
     loads = [pltpu.make_async_copy(field.at[:, 0, :], field_in, load_sem.at[0])]
     loads.append(pltpu.make_async_copy(w_first, wf, load_sem.at[1]))
@@ -120,10 +123,11 @@
             device_id_type=MESH,
         ).wait_recv()
 
-    def each_source(fn):
-        for j in range(1, n_chan):
+    def centre_sources(fn):
+        for j in (1, 2, 3):
             fn(1, j)
 
+    def side_sources(fn):
         @pl.when(z > 0)
         def _():
             for j in range(n_chan):
@@ -135,7 +139,7 @@
                 fn(2, j)
 
     def source(j):
-        return lax.rem(c + n_chan - j, n_chan)
+        return place_of[j]
 
     def send_field(dz, j):
         copy(0, dz, j, whole.at[1, mine, :], whole.at[1 - dz, mine, :]).start()
@@ -145,8 +149,6 @@
     def field_arrives(a, j):
         rows = pl.ds(pl.multiple_of(source(j) * own, own), own)
         arrive(0, a, j, whole.at[a, rows, :])
-
-    each_source(field_arrives)
 
     y = lax.rem(lax.broadcasted_iota(jnp.int32, (1, NXY), 1), NY)
 
@@ -164,8 +166,42 @@
     def wide(column):
         return jnp.concatenate([column] * (NXY // 128), axis=1)
 
+    def coupled_arrives(a, j):
+        arrive(5, a, j, cgot.at[a, source(j)])
+
+    half = NXY // 2
+
+    def convolve(k, a, q):
+        depth = slice(a * 9 * HALF, (a + 1) * 9 * HALF)
+        return lax.dot_general(
+            wf[k, depth, :],
+            patches[depth, q * half : (q + 1) * half],
+            (((0,), (0,)), ((), ())),
+            preferred_element_type=F32,
+        )
+
+    def hidden_copy(k, q, j, owner):
+        part = hidden.at[k, q, pl.ds(pl.multiple_of(owner * units, units), units), :]
+        return pltpu.make_async_remote_copy(
+            src_ref=part,
+            dst_ref=part,
+            send_sem=send_sem.at[1 + k, q, j],
+            recv_sem=recv_sem.at[1 + k, q, j],
+            device_id=peer(0, 1 if j == 3 else j),
+            device_id_type=MESH,
+        )
+
     for k in range(STEPS):
-        for a in range(3):
+        arrivals = coupled_arrives if k else field_arrives
+        rows = pl.ds(pl.multiple_of(c * units, units), units)
+        for a in (1, 0, 2):
+            if a == 1:
+                centre_sources(arrivals)
+            if a == 0:
+                if k == 0:
+                    loads[1].wait()
+                totals = [convolve(k, 1, q) + wide(bias1[k])[:, :half] for q in range(2)]
+                side_sources(arrivals)
             if k == 0:
                 plane = whole[a]
             else:
@@ -182,28 +218,30 @@
                 fronts[a] = front
             for e in range(3):
                 xpad[e, a * HALF : (a + 1) * HALF, PAD : PAD + NXY] = keep(front, e).astype(BF16)
-        for a in range(3):
             for b in range(3):
                 for e in range(3):
                     at = ((a * 3 + b) * 3 + e) * HALF
                     patches[at : at + HALF, :] = xpad[e, a * HALF : (a + 1) * HALF, shifted(b, e)]
-        if k == 0:
-            loads[1].wait()
-        total = lax.dot_general(
-            wf[k], patches[...], (((0,), (0,)), ((), ())), preferred_element_type=F32
-        )
-        rows = pl.ds(pl.multiple_of(c * units, units), units)
-        hidden[k, rows, :] = jnp.maximum(total + wide(bias1[k]), 0.0).astype(BF16)
-        for j in range(1, n_chan):
-            copy(1 + k, 0, j, hidden.at[k, rows, :], hidden.at[k, rows, :]).start()
+        for q in range(2):
+            one = totals[q] + convolve(k, 0, q) + convolve(k, 2, q)
+            hidden[k, q, rows, :] = jnp.maximum(one, 0.0).astype(BF16)
+            for j in (2, 1):
+                hidden_copy(k, q, j, c).start()
         if k == 0:
             for load in loads[2:]:
                 load.wait()
-        summed = jnp.dot(wm[k, :, rows], hidden[k, rows, :], preferred_element_type=F32)
-        for j in range(1, n_chan):
-            theirs = pl.ds(pl.multiple_of(source(j) * units, units), units)
-            arrive(1 + k, 1, j, hidden.at[k, theirs, :])
-            summed += jnp.dot(wm[k, :, theirs], hidden[k, theirs, :], preferred_element_type=F32)
+        sums = []
+        for q in range(2):
+            summed = jnp.dot(wm[k, :, rows], hidden[k, q, rows, :], preferred_element_type=F32)
+            for j in (1, 2, 3):
+                theirs = pl.ds(pl.multiple_of(source(j) * units, units), units)
+                here = hidden.at[k, q, theirs, :]
+                arrive(1 + k, q, j, here)
+                if j == 2:
+                    hidden_copy(k, q, 3, source(2)).start()
+                summed += jnp.dot(wm[k, :, theirs], here[...], preferred_element_type=F32)
+            sums.append(summed)
+        summed = jnp.concatenate(sums, axis=1)
         two = jnp.maximum(summed + wide(bias2[k]), 0.0)
         for e in range(3):
             hpad[e, :, PAD : PAD + NXY] = keep(two, e).astype(BF16)
@@ -221,7 +259,7 @@
                 ).astype(BF16)
 
         def send_parts(dz, j):
-            to = lax.rem(c + j, n_chan)
+            to = place_of[j]
             copy(3 + k, dz, j, psend.at[k, to, 1 - dz], precv.at[k, 1 - dz, c]).start()
 
         each_peer(send_parts)
@@ -230,9 +268,10 @@
         def parts_arrive(a, j):
             arrive(3 + k, a, j, precv.at[k, a, source(j)])
 
-        each_source(parts_arrive)
+        centre_sources(parts_arrive)
+        side_sources(parts_arrive)
         net = precv[k, 1, 0].astype(F32)
-        for a in range(3):
+        for a in (1, 0, 2):
             for s in range(n_chan):
                 if (a, s) != (1, 0):
                     net = net + precv[k, a, s].astype(F32)
@@ -276,12 +315,6 @@
             jnp.int32, (share, share), 1
         )
         logscale[k] = jnp.sum(jnp.where(diagonal, means, 0.0), axis=0, keepdims=True)
-        if k == 0:
-
-            def coupled_arrives(a, j):
-                arrive(5, a, j, cgot.at[a, source(j)])
-
-            each_source(coupled_arrives)
 
     for i in range(2):
         sender = 2 * (c - n_chan // 2) + i
@@ -308,12 +341,12 @@
 
     each_peer(lambda dz, j: copy(0, dz, j, whole.at[1, mine, :], whole.at[1 - dz, mine, :]).wait_send())
     for k in range(STEPS):
-        rows = pl.ds(pl.multiple_of(c * units, units), units)
-        for j in range(1, n_chan):
-            copy(1 + k, 0, j, hidden.at[k, rows, :], hidden.at[k, rows, :]).wait_send()
+        for q in range(2):
+            for j in (1, 2, 3):
+                hidden_copy(k, q, j, source(2) if j == 3 else c).wait_send()
         each_peer(
             lambda dz, j: copy(
-                3 + k, dz, j, psend.at[k, lax.rem(c + j, n_chan), 1 - dz], precv.at[k, 1 - dz, c]
+                3 + k, dz, j, psend.at[k, place_of[j], 1 - dz], precv.at[k, 1 - dz, c]
             ).wait_send()
         )
     each_peer(lambda dz, j: copy(5, dz, j, csend, cgot.at[1 - dz, c]).wait_send())
@@ -352,7 +385,7 @@
             pltpu.VMEM((3, C, NXY), BF16),
             pltpu.VMEM((3, 3 * HALF, NXY + 2 * PAD), BF16),
             pltpu.VMEM((27 * HALF, NXY), BF16),
-            pltpu.VMEM((STEPS, n_chan * units, NXY), BF16),
+            pltpu.VMEM((STEPS, 2, n_chan * units, NXY // 2), BF16),
             pltpu.VMEM((3, units, NXY + 2 * PAD), BF16),
             pltpu.VMEM((9 * units, NXY), BF16),
             pltpu.VMEM((STEPS, n_chan, 3, 2 * share, NXY), BF16),
@@ -369,7 +402,7 @@
             pltpu.SemaphoreType.DMA,
         ],
         compiler_params=pltpu.CompilerParams(
-            collective_id=0, has_side_effects=True, vmem_limit_bytes=48 << 20
+            collective_id=0, has_side_effects=True, vmem_limit_bytes=62 << 20
         ),
     )(
         field, order, jnp.swapaxes(w_first, 1, 2), b_first, w_middle, b_middle,

time: 46 us -> 42.1 us (0.915)
  local copies, waits for them, and re-layouts: 5.75 us -> 1.94 us
    unnamed x18 -> x4, local copies, waits for them, and re-layouts: 5.75 us -> 1.94 us
where the time goes in v2:
time: 42.1 us; the launch traced here: 41.9 us
  Pallas kernels  39.3 us (93%)
  local copies, waits for them, and re-layouts  1.94 us (5%)
  between operations  0.65 us (2%)
    pallas_call x1, Pallas kernels, local(): pl.pallas_call(kernel, out_shape=(jax.ShapeDtypeStruct(field.shape, F32),...  39.3 us
    unnamed x4, local copies, waits for them, and re-layouts  1.94 us

profile of v2, /device:TPU:0, one launch (start us, length us, event | category | flops | bytes accessed | tf_op | source)
XLA Modules:
  0.0 41.9 jit_solution(14731767337581696088)
XLA Ops:
  0.6 39.3 %shard_map.95 = (f32[16,1,512]{2,1,0:T(1,128)}, f32[2,1,8]{2,1,0:T(1,128)}) custom-call(f32[16,1,512]{2,1,0:T(1,128)} %field.1, s32[2,64]{1,0:T(2,128)} %order.1, bf16[2,864,128]{2,1,0:T(8,128)(2,1)} %bitcast.6, bf16[2,128]{1,0:T(2,128)(2,1)} %b_first.1, bf16[2,128,512]{2,1,0:T(8,128)(2,1)} %w_middle.1, bf16[2,128]{1,0:T(2,128)(2,1)} %b_middle.1, ...), custom_call_target="tpu_custom_call" | custom-call | tf_op jit(solution)/shard_map/pallas_call | solution.py:368
  40.0 0.0 copy-start
  40.0 1.4 %copy.13 = f32[16,1,512]{2,1,0:T(1,128)} copy(f32[16,1,512]{2,1,0:T(1,128)} %get-tuple-element.10) | data formatting | bytes 65536
  41.4 0.0 copy-done
  41.4 0.6 %copy.14 = f32[2,8,1]{1,2,0:T(1,128)} copy(f32[2,8,1]{1,2,0:T(1,128)S(1)} %bitcast.7) | data formatting | bytes 128
Async XLA Ops:
  40.0 1.4 %copy-start = (f32[2,1,8]{2,1,0:T(1,128)S(1)}, f32[2,1,8]{2,1,0:T(1,128)}, u32[]{:S(2)}) copy-start(f32[2,1,8]{2,1,0:T(1,128)} %get-tuple-element.5) | copy-start | bytes 196

commit v3 on v2

--- a/solution.py
+++ b/solution.py
@@ -233,14 +233,14 @@
         sums = []
         for q in range(2):
             summed = jnp.dot(wm[k, :, rows], hidden[k, q, rows, :], preferred_element_type=F32)
-            for j in (1, 2, 3):
-                theirs = pl.ds(pl.multiple_of(source(j) * units, units), units)
-                here = hidden.at[k, q, theirs, :]
-                arrive(1 + k, q, j, here)
-                if j == 2:
-                    hidden_copy(k, q, 3, source(2)).start()
-                summed += jnp.dot(wm[k, :, theirs], here[...], preferred_element_type=F32)
             sums.append(summed)
+        for q, j in ((0, 1), (0, 2), (1, 1), (1, 2), (0, 3), (1, 3)):
+            theirs = pl.ds(pl.multiple_of(source(j) * units, units), units)
+            here = hidden.at[k, q, theirs, :]
+            arrive(1 + k, q, j, here)
+            if j == 2:
+                hidden_copy(k, q, 3, source(2)).start()
+            sums[q] += jnp.dot(wm[k, :, theirs], here[...], preferred_element_type=F32)
         summed = jnp.concatenate(sums, axis=1)
         two = jnp.maximum(summed + wide(bias2[k]), 0.0)
         for e in range(3):

time: 42.1 us -> 41.9 us (level)
  no operation moved by 1% of the time
where the time goes in v3:
time: 41.9 us; the launch traced here: 41.7 us
  Pallas kernels  39.1 us (93%)
  local copies, waits for them, and re-layouts  1.94 us (5%)
  between operations  0.65 us (2%)
    pallas_call x1, Pallas kernels, local(): pl.pallas_call(kernel, out_shape=(jax.ShapeDtypeStruct(field.shape, F32),...  39.1 us
    unnamed x4, local copies, waits for them, and re-layouts  1.94 us

profile of v3, /device:TPU:0, one launch (start us, length us, event | category | flops | bytes accessed | tf_op | source)
XLA Modules:
  0.0 41.7 jit_solution(13185249731338590115)
XLA Ops:
  0.6 39.1 %shard_map.95 = (f32[16,1,512]{2,1,0:T(1,128)}, f32[2,1,8]{2,1,0:T(1,128)}) custom-call(f32[16,1,512]{2,1,0:T(1,128)} %field.1, s32[2,64]{1,0:T(2,128)} %order.1, bf16[2,864,128]{2,1,0:T(8,128)(2,1)} %bitcast.6, bf16[2,128]{1,0:T(2,128)(2,1)} %b_first.1, bf16[2,128,512]{2,1,0:T(8,128)(2,1)} %w_middle.1, bf16[2,128]{1,0:T(2,128)(2,1)} %b_middle.1, ...), custom_call_target="tpu_custom_call" | custom-call | tf_op jit(solution)/shard_map/pallas_call | solution.py:368
  39.8 0.0 copy-start
  39.8 1.4 %copy.13 = f32[16,1,512]{2,1,0:T(1,128)} copy(f32[16,1,512]{2,1,0:T(1,128)} %get-tuple-element.10) | data formatting | bytes 65536
  41.2 0.0 copy-done
  41.2 0.6 %copy.14 = f32[2,8,1]{1,2,0:T(1,128)} copy(f32[2,8,1]{1,2,0:T(1,128)S(1)} %bitcast.7) | data formatting | bytes 128
Async XLA Ops:
  39.8 1.4 %copy-start = (f32[2,1,8]{2,1,0:T(1,128)S(1)}, f32[2,1,8]{2,1,0:T(1,128)}, u32[]{:S(2)}) copy-start(f32[2,1,8]{2,1,0:T(1,128)} %get-tuple-element.5) | copy-start | bytes 196
